TPU v7x, 32 devices: a whole 2x2x4 slice. The times are simulated.
32 devices in a mesh: pair: 8 (over z, y), band: 4 (over x, core).
Axes of the slice: x: 2, y: 2, z: 4, core: 2. Of those that a mesh axis runs over, the one named last changes fastest.
Arguments:
- orbitals: bfloat16 [2048, 23, 64], P('pair'), may hold values from -6 to 6
- screening: bfloat16 [1024, 8, 1024], P('pair', None, 'band'), may hold values from -0.1875 to 0.1875
- trial: bfloat16 [1024, 23, 64], P('pair'), may hold values from -6 to 6
- pair_kpts: int32 [8, 2], replicated, may hold values from 0 to 22
- pair_q: int32 [8], replicated, may hold values from 0 to 7
Outputs:
- applied: float32 [1024, 23, 64], P('pair', None, 'band')
All inputs are finite; a program needn't handle non-finite values.
Results may differ from a plain program's by a relative error of at most 0.013.
Values may be sent and summed in bfloat16 or wider, within the bound.
No kernel may reach another device: no remote copies, remote signals or barrier semaphores. Data moves between devices by JAX's collectives and lax.ppermute only.
A program may use at most 64 MiB of HBM per device.

v0:
```python
import math
import jax
import jax.numpy as jnp
from jax import lax
from jax.sharding import PartitionSpec as P

NV = 32
NC = 32
NR = 2048
NG = 1024
KPTS = 23
NB = 64


def basis_rows(first_row, row_count, point_count):
    frequency = first_row + jnp.arange(row_count, dtype=jnp.int32)
    position = jnp.arange(point_count, dtype=jnp.int32)
    phase_index = (2 * position[None, :] + 1) * frequency[:, None] % (4 * point_count)
    values = jnp.cos(phase_index.astype(jnp.float32) * (math.pi / (2 * point_count))) * math.sqrt(
        2.0 / point_count
    )
    return values.astype(jnp.bfloat16)


def densities(first_set, second_set):
    merged = first_set.astype(jnp.float32)[:, :, None] * second_set.astype(jnp.float32)[:, None, :]
    return merged.reshape(first_set.shape[0], first_set.shape[1] * second_set.shape[1]).astype(
        jnp.bfloat16
    )


def transform(basis_block, first_set, second_set):
    return lax.dot_general(
        basis_block,
        densities(first_set, second_set),
        (((1,), (0,)), ((), ())),
        preferred_element_type=jnp.float32,
    ).astype(jnp.bfloat16)


def on_device(orbitals, screening, trial, pair_kpts, pair_q):
    band_count = lax.axis_size("band")
    pair_count = lax.axis_size("pair")
    pair_here = lax.axis_index("pair")
    own_kpts = lax.dynamic_index_in_dim(pair_kpts, pair_here, 0, keepdims=False)
    listed = pair_kpts.shape[0]
    vector_count = trial.shape[2]
    orbital_send = orbitals[:, pair_kpts].reshape(orbitals.shape[0], listed, 2 * NB)
    trial_send = trial[:, pair_kpts].reshape(trial.shape[0], listed, 2 * vector_count)
    screen_send = screening[:, pair_q]
    orbital_got, trial_got, screen_got = (
        lax.all_to_all(orbital_send, "pair", split_axis=1, concat_axis=0, tiled=True),
        lax.all_to_all(trial_send, "pair", split_axis=1, concat_axis=0, tiled=True),
        lax.all_to_all(screen_send, "pair", split_axis=1, concat_axis=0, tiled=True),
    )
    screen_cols = screen_got[:, 0]
    first_orb = orbital_got[:, 0, :NB]
    second_orb = orbital_got[:, 0, NB:]
    row_count = NG // band_count
    basis_block = basis_rows(lax.axis_index("band") * row_count, row_count, NR)
    valence = transform(basis_block, first_orb[:, :NV], second_orb[:, :NV])
    conduction = transform(basis_block, first_orb[:, NV:], second_orb[:, NV:])
    screened = lax.dot_general(
        screen_cols,
        lax.all_gather(valence, "band", axis=0, tiled=True),
        (((0,), (0,)), ((), ())),
        preferred_element_type=jnp.float32,
    ).astype(jnp.bfloat16)
    raw = lax.dot_general(
        conduction, screened, (((0,), (0,)), ((), ())), preferred_element_type=jnp.float32
    ) * (1.0 / math.sqrt(NG))
    kernel = (
        raw.reshape(NC, NC, NV, NV)
        .transpose(2, 0, 3, 1)
        .reshape(NV * NC, NV * NC)
        .astype(jnp.bfloat16)
    )
    trial_first = trial_got[:, 0, :vector_count]
    trial_second = trial_got[:, 0, vector_count:]
    apply_scale = 1.0 / math.sqrt(NV * NC)
    forward = (
        lax.dot_general(
            kernel, trial_second, (((1,), (0,)), ((), ())), preferred_element_type=jnp.float32
        )
        * apply_scale
    )
    backward = (
        lax.dot_general(
            kernel, trial_first, (((0,), (0,)), ((), ())), preferred_element_type=jnp.float32
        )
        * apply_scale
    )
    partials = jnp.stack([forward, backward])
    summed = lax.psum_scatter(
        partials.astype(jnp.bfloat16), "band", scatter_dimension=2, tiled=True
    ).astype(jnp.float32)
    share = summed.shape[2]
    state_rows = summed.shape[1] // pair_count
    kpt_ids = jnp.arange(KPTS, dtype=jnp.int32)
    one_hot = (own_kpts[:, None] == kpt_ids[None, :]).astype(jnp.float32)
    spread = (
        summed[0][:, None, :] * one_hot[0][None, :, None]
        + summed[1][:, None, :] * one_hot[1][None, :, None]
    )
    spread = spread.reshape(summed.shape[1], KPTS * share)
    scattered = lax.psum_scatter(spread, "pair", scatter_dimension=0, tiled=True)
    return scattered.reshape(state_rows, KPTS, share)


def solution(mesh):
    return jax.shard_map(
        on_device,
        mesh=mesh,
        in_specs=(P("pair", None, None), P("pair", None, "band"), P("pair", None, None), P(), P()),
        out_specs=P("pair", None, "band"),
        check_vma=False,
    )
```

profile of v0, /device:TPU:0, one launch (start us, length us, event | category | flops | bytes accessed | tf_op | source)
XLA Modules:
  0.0 212.1 jit_solution(7176523066295668518)
XLA Ops:
  6.5 0.0 copy-start
  6.5 0.8 compare_select_fusion
  7.3 0.1 copy.25
  7.4 0.1 reshape.56
  7.5 0.2 copy-done
  7.7 1.4 gather_fusion
  9.1 7.3 %all-to-all-start = ((bf16[256,8,128]{0,2,1:T(8,128)(2,1)}), bf16[256,8,128]{0,2,1:T(8,128)(2,1)S(1)}, u32[]{:S(2)}, u32[]{:S(2)}) async-start(bf16[256,8,128]{0,2,1:T(8,128)(2,1)} %bitcast.2), calls=%async_computation | async-start | bytes 1048576 | tf_op jit(solution)/shard_map/all_to_all | solution.py:52
  16.4 0.0 all-gather.2.cloned.1.call-start
  16.4 14.4 %all-to-all-done = bf16[256,8,128]{0,2,1:T(8,128)(2,1)S(1)} async-done(((bf16[256,8,128]{0,2,1:T(8,128)(2,1)}), bf16[256,8,128]{0,2,1:T(8,128)(2,1)S(1)}, u32[]{:S(2)}, u32[]{:S(2)}) %all-to-all-start) | async-done | bytes 524320 | tf_op jit(solution)/shard_map/all_to_all | solution.py:52
  30.9 0.3 copy.26
  31.1 0.2 fusion.23
  31.3 0.2 copy.28
  31.6 0.2 copy.27
  31.8 4.2 %multiply_convert_fusion = (bf16[2048,32,32]{0,2,1:T(8,128)(2,1)S(1)}, bf16[2048,32,32]{0,2,1:T(8,128)(2,1)}) fusion(f32[2048,32]{0,1:T(8,128)S(1)} %get-tuple-element.9, f32[2048,32]{0,1:T(8,128)S(1)} %get-tuple-element.7, f32[2048,32]{0,1:T(8,128)S(1)} %get-tuple-element.10, f32[2048,32]{0,1:T(8,128)S(1)} %get-tuple-element.8), kind=kLoop, calls=%fused_computation.3 | loop fusion | flops 8388608 | bytes 9437184 | tf_op jit(solution)/shard_map/convert_element_type | solution.py:27
  36.0 0.0 copy-start.2
  36.0 10.2 %convolution_convert_fusion.1 = bf16[256,1024]{1,0:T(8,128)(2,1)} fusion(bf16[2048,1024]{0,1:T(8,128)(2,1)S(1)} %bitcast.70, s32[256]{0:T(256)S(1)} %iota_add_fusion, s32[2048]{0:T(1024)S(1)} %multiply_add_fusion), kind=kOutput, calls=%fused_computation.21 | convolution fusion | flops 1082392576 | bytes 4727808 | tf_op jit(solution)/shard_map/dot_general | solution.py:33
  46.2 0.0 copy-start.5
  46.2 0.0 copy-start.1
  46.2 0.0 all-gather.2.cloned.1.call-update
  46.3 0.0 copy-done.2
  46.3 1.3 gather_fusion.2
  47.6 3.6 %all-to-all-start.2 = ((bf16[128,8,128]{0,2,1:T(8,128)(2,1)}), bf16[128,8,128]{0,2,1:T(8,128)(2,1)S(1)}, u32[]{:S(2)}, u32[]{:S(2)}) async-start(bf16[128,8,128]{0,2,1:T(8,128)(2,1)} %bitcast.17), calls=%async_computation.2 | async-start | bytes 524288 | tf_op jit(solution)/shard_map/all_to_all | solution.py:53
  51.2 0.0 copy-done.5
  51.3 0.0 copy-done.1
  51.3 2.0 gather_fusion.1
  53.3 0.9 copy.29
  54.2 6.1 %all-to-all-done.2 = bf16[128,8,128]{0,2,1:T(8,128)(2,1)S(1)} async-done(((bf16[128,8,128]{0,2,1:T(8,128)(2,1)}), bf16[128,8,128]{0,2,1:T(8,128)(2,1)S(1)}, u32[]{:S(2)}, u32[]{:S(2)}) %all-to-all-start.2) | async-done | bytes 262176 | tf_op jit(solution)/shard_map/all_to_all | solution.py:53
  60.3 3.6 %all-to-all-start.1 = ((bf16[128,8,256]{2,0,1:T(8,128)(2,1)}), bf16[128,8,256]{2,0,1:T(8,128)(2,1)S(1)}, u32[]{:S(2)}, u32[]{:S(2)}) async-start(bf16[128,8,256]{2,0,1:T(8,128)(2,1)} %copy.29), calls=%async_computation.1 | async-start | bytes 1048576 | tf_op jit(solution)/shard_map/all_to_all | solution.py:54
  63.9 0.2 reduce-scatter.3.cloned.1.call-start
  64.1 0.2 copy.31
  64.3 11.5 %convolution_convert_fusion.2 = bf16[256,1024]{1,0:T(8,128)(2,1)} fusion(bf16[2048,1024]{0,1:T(8,128)(2,1)} %bitcast.69, s32[256]{0:T(256)S(1)} %iota_add_fusion, s32[2048]{0:T(1024)S(1)} %multiply_add_fusion), kind=kOutput, calls=%fused_computation.22 | convolution fusion | flops 1082392576 | bytes 4727808 | tf_op jit(solution)/shard_map/dot_general | solution.py:33
  75.8 2.3 %all-to-all-done.1 = bf16[128,8,256]{2,0,1:T(8,128)(2,1)S(1)} async-done(((bf16[128,8,256]{2,0,1:T(8,128)(2,1)}), bf16[128,8,256]{2,0,1:T(8,128)(2,1)S(1)}, u32[]{:S(2)}, u32[]{:S(2)}) %all-to-all-start.1) | async-done | bytes 524320 | tf_op jit(solution)/shard_map/all_to_all | solution.py:54
  78.1 0.0 copy-start.3
  78.1 0.0 all-gather.2.cloned.1.call-done
  78.1 0.8 copy-done.3
  78.9 3.3 %multiply_convert_fusion.2 = bf16[1024,1024]{1,0:T(8,128)(2,1)S(1)} fusion(bf16[256,1024]{1,0:T(8,128)(2,1)} %convolution_convert_fusion.2, bf16[1024,256]{1,0:T(8,128)(2,1)} %bitcast.78, bf16[1024,1024]{1,0:T(8,128)(2,1)} %all-gather.2.cloned.1.call-done), kind=kOutput, calls=%fused_computation.5 | convolution fusion | flops 1076101120 | bytes 5242880 | tf_op jit(solution)/shard_map/dot_general | solution.py:69
  82.2 8.2 %convert_element_type.73 = bf16[32,32,32,32]{3,2,1,0:T(8,128)(2,1)} reshape(bf16[1024,1024]{1,0:T(8,128)(2,1)S(1)} %multiply_convert_fusion.2) | data formatting | bytes 4194304 | tf_op jit(solution)/shard_map/convert_element_type | solution.py:76
  90.4 15.2 %copy.30 = bf16[32,32,32,32]{1,3,0,2:T(8,128)(2,1)} copy(bf16[32,32,32,32]{3,2,1,0:T(8,128)(2,1)} %convert_element_type.73) | data formatting | bytes 4194304 | tf_op jit(solution)/shard_map/convert_element_type | solution.py:76
  105.6 11.3 %convert_element_type.75 = bf16[1024,1024]{1,0:T(8,128)(2,1)S(1)} reshape(bf16[32,32,32,32]{3,2,1,0:T(8,128)(2,1)} %bitcast.67) | data formatting | bytes 4194304 | tf_op jit(solution)/shard_map/convert_element_type | solution.py:76
  116.9 0.8 fusion.10
  117.7 0.0 copy-start.4
  117.8 0.5 fusion.9
  118.3 0.7 pad_maximum_fusion
  119.0 0.0 reduce-scatter.3.cloned.1.call-update
  119.0 0.0 reduce-scatter.5.cloned.1.call-start
  119.1 0.0 copy-done.4
  119.1 0.2 dynamic-slice_reduce_fusion
  119.3 0.1 compare_convert_fusion
  119.4 0.1 mul.153
  119.4 0.1 mul.154
  119.5 0.1 mul.161
  119.6 0.1 mul.162
  119.7 18.6 %reduce-scatter.3.cloned.1.call-done = bf16[2,1024,16]{1,2,0:T(8,128)(2,1)} async-done(((bf16[2,1024,64]{1,2,0:T(8,128)(2,1)}), bf16[2,1024,16]{1,2,0:T(8,128)(2,1)}) %reduce-scatter.3.cloned.1.call-update) | async-done | bytes 65552 | tf_op jit(solution)/shard_map/reduce_scatter | solution.py:94
  138.3 0.8 convert_element_type.76
  139.2 1.4 fusion.6
  140.5 0.0 reduce-scatter.5.cloned.1.call-update
  140.6 65.0 %reduce-scatter.5.cloned.1.call-done = f32[128,368]{0,1:T(8,128)} async-done(((f32[1024,368]{0,1:T(8,128)}), f32[128,368]{0,1:T(8,128)}) %reduce-scatter.5.cloned.1.call-update) | async-done | bytes 188432 | tf_op jit(solution)/shard_map/reduce_scatter | solution.py:106
  (9 shorter events, 0.1 us)
Async XLA Ops:
  6.5 1.1 copy-start
  9.1 21.8 %all-to-all-start = ((bf16[256,8,128]{0,2,1:T(8,128)(2,1)}), bf16[256,8,128]{0,2,1:T(8,128)(2,1)S(1)}, u32[]{:S(2)}, u32[]{:S(2)}) async-start(bf16[256,8,128]{0,2,1:T(8,128)(2,1)} %bitcast.2), calls=%async_computation | async-start | bytes 1048576 | tf_op jit(solution)/shard_map/all_to_all | solution.py:52
  16.4 61.8 %all-gather.2.cloned.1.call-start = ((), (), s32[]{:S(2)}) async-start(), calls=%async_computation.5 | async-start | bytes 2621440 | tf_op jit(solution)/shard_map/all_gather | solution.py:65
  36.0 10.2 %copy-start.2 = (bf16[128,23,64]{0,2,1:T(8,128)(2,1)S(1)}, bf16[128,23,64]{0,2,1:T(8,128)(2,1)}, u32[]{:S(2)}) copy-start(bf16[128,23,64]{0,2,1:T(8,128)(2,1)} %param.7) | copy-start | bytes 1130500
  46.2 5.0 %copy-start.5 = (s32[8]{0:T(128)S(1)}, s32[8]{0:T(128)}, u32[]{:S(2)}) copy-start(s32[8]{0:T(128)} %param.9) | copy-start | bytes 100
  46.2 5.0 %copy-start.1 = (bf16[128,8,256]{2,1,0:T(8,128)(2,1)S(1)}, bf16[128,8,256]{2,1,0:T(8,128)(2,1)}, u32[]{:S(2)}) copy-start(bf16[128,8,256]{2,1,0:T(8,128)(2,1)} %param.6) | copy-start | bytes 1572868
  47.6 12.7 %all-to-all-start.2 = ((bf16[128,8,128]{0,2,1:T(8,128)(2,1)}), bf16[128,8,128]{0,2,1:T(8,128)(2,1)S(1)}, u32[]{:S(2)}, u32[]{:S(2)}) async-start(bf16[128,8,128]{0,2,1:T(8,128)(2,1)} %bitcast.17), calls=%async_computation.2 | async-start | bytes 524288 | tf_op jit(solution)/shard_map/all_to_all | solution.py:53
  60.3 17.8 %all-to-all-start.1 = ((bf16[128,8,256]{2,0,1:T(8,128)(2,1)}), bf16[128,8,256]{2,0,1:T(8,128)(2,1)S(1)}, u32[]{:S(2)}, u32[]{:S(2)}) async-start(bf16[128,8,256]{2,0,1:T(8,128)(2,1)} %copy.29), calls=%async_computation.1 | async-start | bytes 1048576 | tf_op jit(solution)/shard_map/all_to_all | solution.py:54
  63.9 74.4 %reduce-scatter.3.cloned.1.call-start = ((), (), s32[]{:S(2)}) async-start(), calls=%async_computation.6 | async-start | bytes 327680 | tf_op jit(solution)/shard_map/reduce_scatter | solution.py:94
  78.1 0.8 copy-start.3
  117.7 1.3 copy-start.4
  119.0 86.5 %reduce-scatter.5.cloned.1.call-start = ((), (), s32[]{:S(2)}) async-start(), calls=%async_computation.7 | async-start | bytes 1695744 | tf_op jit(solution)/shard_map/reduce_scatter | solution.py:106
Sparse Core Ops, SparseCore 0:
  46.4 21.6 all-gather.1
  119.1 19.1 reduce-scatter.2
  141.7 63.7 reduce-scatter.4
where the time goes:
time: 213 us; the launch traced here: 212 us
  waiting for transfers between devices  106 us (50%)
  local copies, waits for them, and re-layouts  43.1 us (20%)
  matrix products  26.3 us (12%)
  starting transfers between devices  14.8 us (7%)
  between operations  13.3 us (6%)
  other arithmetic  8.09 us (4%)
    reduce_scatter x1, waiting for transfers between devices, on_device(): lax.psum_scatter(spread, 'pair', scatter_dimension=0, tiled=True)  65 us
    convert_element_type x3, local copies, waits for them, and re-layouts, on_device(): kernel = raw.reshape(NC, NC, NV, NV).transpose(2, 0, 3, 1).reshape(NV * N...  34.7 us
    dot_general x2, matrix products, transform(): lax.dot_general(basis_block, densities(first_set, second_set), (((1,), (0...  21.7 us
    reduce_scatter x1, waiting for transfers between devices, on_device(): lax.psum_scatter(partials.astype(jnp.bfloat16), 'band', scatter_dimension...  18.6 us
    all_to_all x1, waiting for transfers between devices, on_device(): lax.all_to_all(orbital_send, 'pair', split_axis=1, concat_axis=0, tiled=T...  14.4 us
    all_to_all x1, starting transfers between devices, on_device(): lax.all_to_all(orbital_send, 'pair', split_axis=1, concat_axis=0, tiled=T...  7.31 us
    all_to_all x1, waiting for transfers between devices, on_device(): lax.all_to_all(trial_send, 'pair', split_axis=1, concat_axis=0, tiled=True)  6.1 us
  transfers between devices with their start and end apart: 6, of which 5 were waited for; matrix products, arithmetic and copies ran while one was open for 8% of the time, Pallas kernels for 0%

commit v1 on v0

--- a/solution.py
+++ b/solution.py
@@ -10,6 +10,22 @@
 NG = 1024
 KPTS = 23
 NB = 64
+
+
+def exchange_in_pairs(array, axis, split, join):
+    ways, here = (lax.axis_size(axis), lax.axis_index(axis))
+    width = array.shape[split] // ways
+    shape = list(array.shape)
+    shape[split] = width
+    height = shape[join]
+    shape[join] = height * ways
+    full = jnp.zeros(shape, array.dtype)
+    for mask in range(ways):
+        part = lax.dynamic_slice_in_dim(array, (here ^ mask) * width, width, axis=split)
+        if mask:
+            part = lax.ppermute(part, axis, [(d, d ^ mask) for d in range(ways)])
+        full = lax.dynamic_update_slice_in_dim(full, part, (here ^ mask) * height, axis=join)
+    return full
 
 
 def basis_rows(first_row, row_count, point_count):
@@ -49,7 +65,7 @@
     trial_send = trial[:, pair_kpts].reshape(trial.shape[0], listed, 2 * vector_count)
     screen_send = screening[:, pair_q]
     orbital_got, trial_got, screen_got = (
-        lax.all_to_all(orbital_send, "pair", split_axis=1, concat_axis=0, tiled=True),
+        exchange_in_pairs(orbital_send, "pair", 1, 0),
         lax.all_to_all(trial_send, "pair", split_axis=1, concat_axis=0, tiled=True),
         lax.all_to_all(screen_send, "pair", split_axis=1, concat_axis=0, tiled=True),
     )

time: 213 us -> 206 us (0.967)
  waiting for transfers between devices: 106 us -> 98.7 us
  starting transfers between devices: 14.8 us -> 20.4 us
    all_to_all x1 -> x0, waiting for transfers between devices: 14.4 us -> none  [on_device(): lax.all_to_all(orbital_send, 'pair', split_axis=1, concat_axis=0, tiled=T...]
    ppermute x0 -> x7, starting transfers between devices: none -> 12.6 us  [exchange_in_pairs(): part = lax.ppermute(part, axis, [(d, d ^ mask) for d in range(ways)])]
    all_to_all x1 -> x0, starting transfers between devices: 7.31 us -> none  [on_device(): lax.all_to_all(orbital_send, 'pair', split_axis=1, concat_axis=0, tiled=T...]
    ppermute x0 -> x7, waiting for transfers between devices: none -> 6.94 us  [exchange_in_pairs(): part = lax.ppermute(part, axis, [(d, d ^ mask) for d in range(ways)])]
  transfers between devices with their start and end apart: 6 -> 12, of which waited for: 5 -> 6; matrix products, arithmetic and copies ran while one was open for 8% -> 8% of each run, Pallas kernels for 0% -> 0%
where the time goes in v1:
time: 206 us; the launch traced here: 205 us
  waiting for transfers between devices  98.7 us (48%)
  local copies, waits for them, and re-layouts  41.3 us (20%)
  matrix products  25.1 us (12%)
  starting transfers between devices  20.4 us (10%)
  between operations  13.4 us (7%)
  other arithmetic  6.04 us (3%)
    reduce_scatter x1, waiting for transfers between devices, on_device(): lax.psum_scatter(spread, 'pair', scatter_dimension=0, tiled=True)  64.9 us
    convert_element_type x3, local copies, waits for them, and re-layouts, on_device(): kernel = raw.reshape(NC, NC, NV, NV).transpose(2, 0, 3, 1).reshape(NV * N...  34.5 us
    dot_general x2, matrix products, transform(): lax.dot_general(basis_block, densities(first_set, second_set), (((1,), (0...  20.4 us
    reduce_scatter x1, waiting for transfers between devices, on_device(): lax.psum_scatter(partials.astype(jnp.bfloat16), 'band', scatter_dimension...  18.7 us
    ppermute x7, starting transfers between devices, exchange_in_pairs(): part = lax.ppermute(part, axis, [(d, d ^ mask) for d in range(ways)])  12.6 us
    ppermute x7, waiting for transfers between devices, exchange_in_pairs(): part = lax.ppermute(part, axis, [(d, d ^ mask) for d in range(ways)])  6.94 us
    all_to_all x1, waiting for transfers between devices, on_device(): lax.all_to_all(trial_send, 'pair', split_axis=1, concat_axis=0, tiled=True)  5.69 us
  transfers between devices with their start and end apart: 12, of which 6 were waited for; matrix products, arithmetic and copies ran while one was open for 8% of the time, Pallas kernels for 0%

profile of v1, /device:TPU:0, one launch (start us, length us, event | category | flops | bytes accessed | tf_op | source)
XLA Modules:
  0.0 204.9 jit_solution(2601034642887058930)
XLA Ops:
  6.5 0.0 copy-start
  6.5 0.0 all-gather.2.cloned.1.call-start
  6.5 0.8 compare_select_fusion
  7.3 0.1 copy.19
  7.4 0.1 reshape.56
  7.5 0.2 copy-done
  7.7 0.6 gather_fusion
  8.3 0.1 constant_dynamic-slice_fusion.1
  8.4 3.1 %collective-permute-start = (bf16[256,1,128]{0,2,1:T(8,128)(2,1)S(1)}, bf16[256,1,128]{0,2,1:T(8,128)(2,1)S(1)}, u32[]{:S(2)}, u32[]{:S(2)}) collective-permute-start(bf16[256,1,128]{0,2,1:T(8,128)(2,1)S(1)} %get-tuple-element.13), channel_id=1, source_target_pairs={{0,4},{4,0},{8,12},{12,8},{16,20},{20,16},{24,28},{28,24},{1,5},{5... | collective-permute-start | bytes 196616 | tf_op jit(solution)/shard_map/ppermute | solution.py:26
  11.4 1.6 collective-permute-start.1
  13.0 0.0 collective-permute-start.2
  13.0 3.0 %collective-permute-start.3 = (bf16[256,1,128]{0,2,1:T(8,128)(2,1)S(1)}, bf16[256,1,128]{0,2,1:T(8,128)(2,1)S(1)}, u32[]{:S(2)}, u32[]{:S(2)}) collective-permute-start(bf16[256,1,128]{0,2,1:T(8,128)(2,1)S(1)} %get-tuple-element.10), channel_id=1, source_target_pairs={{0,16},{4,20},{8,24},{12,28},{16,0},{20,4},{24,8},{28,12},{1,17},{... | collective-permute-start | bytes 196616 | tf_op jit(solution)/shard_map/ppermute | solution.py:26
  16.0 1.3 collective-permute-start.4
  17.3 0.0 collective-permute-done
  17.3 3.7 %collective-permute-start.5 = (bf16[256,1,128]{0,2,1:T(8,128)(2,1)S(1)}, bf16[256,1,128]{0,2,1:T(8,128)(2,1)S(1)}, u32[]{:S(2)}, u32[]{:S(2)}) collective-permute-start(bf16[256,1,128]{0,2,1:T(8,128)(2,1)S(1)} %get-tuple-element.8), channel_id=1, source_target_pairs={{0,24},{4,28},{8,16},{12,20},{16,8},{20,12},{24,0},{28,4},{1,25},{... | collective-permute-start | bytes 196616 | tf_op jit(solution)/shard_map/ppermute | solution.py:26
  21.0 0.0 collective-permute-done.1
  21.0 0.1 collective-permute-start.6
  21.1 0.0 collective-permute-done.2
  21.1 0.0 collective-permute-done.3
  21.2 5.1 %collective-permute-done.4 = bf16[256,1,128]{0,2,1:T(8,128)(2,1)S(1)} collective-permute-done((bf16[256,1,128]{0,2,1:T(8,128)(2,1)S(1)}, bf16[256,1,128]{0,2,1:T(8,128)(2,1)S(1)}, u32[]{:S(2)}, u32[]{:S(2)}) %collective-permute-start.4) | collective-permute-done | bytes 65568 | tf_op jit(solution)/shard_map/ppermute | solution.py:26
  26.2 0.0 collective-permute-done.5
  26.2 1.9 collective-permute-done.6
  28.2 0.1 slice_convert_fusion
  28.3 1.1 multiply_convert_fusion
  29.3 0.0 copy-start.2
  29.4 10.2 %convolution_convert_fusion.1 = bf16[256,1024]{1,0:T(8,128)(2,1)} fusion(bf16[2048,1024]{0,1:T(8,128)(2,1)S(1)} %bitcast.68, s32[256]{0:T(256)S(1)} %iota_add_fusion, s32[2048]{0:T(1024)S(1)} %multiply_add_fusion), kind=kOutput, calls=%fused_computation.21 | convolution fusion | flops 1082392576 | bytes 4727808 | tf_op jit(solution)/shard_map/dot_general | solution.py:49
  39.6 0.0 all-gather.2.cloned.1.call-update
  39.6 0.0 copy-done.2
  39.6 1.3 gather_fusion.2
  40.9 3.9 %all-to-all-start.1 = ((bf16[128,8,128]{0,2,1:T(8,128)(2,1)}), bf16[128,8,128]{0,2,1:T(8,128)(2,1)S(1)}, u32[]{:S(2)}, u32[]{:S(2)}) async-start(bf16[128,8,128]{0,2,1:T(8,128)(2,1)} %bitcast.16), calls=%async_computation.1 | async-start | bytes 524288 | tf_op jit(solution)/shard_map/all_to_all | solution.py:69
  44.8 0.0 copy-done.5
  44.8 0.0 copy-done.1
  44.8 2.0 gather_fusion.1
  46.9 0.9 copy.20
  47.8 5.7 %all-to-all-done.1 = bf16[128,8,128]{0,2,1:T(8,128)(2,1)S(1)} async-done(((bf16[128,8,128]{0,2,1:T(8,128)(2,1)}), bf16[128,8,128]{0,2,1:T(8,128)(2,1)S(1)}, u32[]{:S(2)}, u32[]{:S(2)}) %all-to-all-start.1) | async-done | bytes 262176 | tf_op jit(solution)/shard_map/all_to_all | solution.py:69
  53.5 3.6 %all-to-all-start = ((bf16[128,8,256]{2,0,1:T(8,128)(2,1)}), bf16[128,8,256]{2,0,1:T(8,128)(2,1)S(1)}, u32[]{:S(2)}, u32[]{:S(2)}) async-start(bf16[128,8,256]{2,0,1:T(8,128)(2,1)} %copy.20), calls=%async_computation | async-start | bytes 1048576 | tf_op jit(solution)/shard_map/all_to_all | solution.py:70
  57.1 0.2 reduce-scatter.3.cloned.1.call-start
  57.3 1.1 multiply_convert_fusion.1
  58.4 10.2 %convolution_convert_fusion.2 = bf16[256,1024]{1,0:T(8,128)(2,1)} fusion(bf16[2048,1024]{0,1:T(8,128)(2,1)S(1)} %bitcast.67, s32[256]{0:T(256)S(1)} %iota_add_fusion, s32[2048]{0:T(1024)S(1)} %multiply_add_fusion), kind=kOutput, calls=%fused_computation.22 | convolution fusion | flops 1082392576 | bytes 4727808 | tf_op jit(solution)/shard_map/dot_general | solution.py:49
  68.6 0.2 copy.22
  68.8 2.5 %all-to-all-done = bf16[128,8,256]{2,0,1:T(8,128)(2,1)S(1)} async-done(((bf16[128,8,256]{2,0,1:T(8,128)(2,1)}), bf16[128,8,256]{2,0,1:T(8,128)(2,1)S(1)}, u32[]{:S(2)}, u32[]{:S(2)}) %all-to-all-start) | async-done | bytes 524320 | tf_op jit(solution)/shard_map/all_to_all | solution.py:70
  71.2 0.8 copy-done.3
  72.0 3.3 %multiply_convert_fusion.2 = bf16[1024,1024]{1,0:T(8,128)(2,1)S(1)} fusion(bf16[256,1024]{1,0:T(8,128)(2,1)} %convolution_convert_fusion.2, bf16[1024,256]{1,0:T(8,128)(2,1)} %bitcast.73, bf16[1024,1024]{1,0:T(8,128)(2,1)} %all-gather.2.cloned.1.call-done), kind=kOutput, calls=%fused_computation.5 | convolution fusion | flops 1076101120 | bytes 5242880 | tf_op jit(solution)/shard_map/dot_general | solution.py:85
  75.3 7.9 %convert_element_type.73 = bf16[32,32,32,32]{3,2,1,0:T(8,128)(2,1)} reshape(bf16[1024,1024]{1,0:T(8,128)(2,1)S(1)} %multiply_convert_fusion.2) | data formatting | bytes 4194304 | tf_op jit(solution)/shard_map/convert_element_type | solution.py:92
  83.3 15.2 %copy.21 = bf16[32,32,32,32]{1,3,0,2:T(8,128)(2,1)} copy(bf16[32,32,32,32]{3,2,1,0:T(8,128)(2,1)} %convert_element_type.73) | data formatting | bytes 4194304 | tf_op jit(solution)/shard_map/convert_element_type | solution.py:92
  98.5 11.3 %convert_element_type.75 = bf16[1024,1024]{1,0:T(8,128)(2,1)S(1)} reshape(bf16[32,32,32,32]{3,2,1,0:T(8,128)(2,1)} %bitcast.65) | data formatting | bytes 4194304 | tf_op jit(solution)/shard_map/convert_element_type | solution.py:92
  109.8 0.8 fusion.10
  110.6 0.0 copy-start.4
  110.6 0.5 fusion.9
  111.1 0.7 pad_maximum_fusion
  111.9 0.0 reduce-scatter.3.cloned.1.call-update
  111.9 0.0 reduce-scatter.5.cloned.1.call-start
  111.9 0.0 copy-done.4
  112.0 0.2 fusion.15
  112.1 0.1 compare_convert_fusion
  112.2 0.1 mul.185
  112.3 0.1 mul.186
  112.4 0.1 mul.193
  112.4 0.1 mul.194
  112.5 18.7 %reduce-scatter.3.cloned.1.call-done = bf16[2,1024,16]{1,2,0:T(8,128)(2,1)} async-done(((bf16[2,1024,64]{1,2,0:T(8,128)(2,1)}), bf16[2,1024,16]{1,2,0:T(8,128)(2,1)}) %reduce-scatter.3.cloned.1.call-update) | async-done | bytes 65552 | tf_op jit(solution)/shard_map/reduce_scatter | solution.py:110
  131.2 0.8 convert_element_type.76
  132.1 1.4 fusion.6
  133.4 0.0 reduce-scatter.5.cloned.1.call-update
  133.5 64.9 %reduce-scatter.5.cloned.1.call-done = f32[128,368]{0,1:T(8,128)} async-done(((f32[1024,368]{0,1:T(8,128)}), f32[128,368]{0,1:T(8,128)}) %reduce-scatter.5.cloned.1.call-update) | async-done | bytes 188432 | tf_op jit(solution)/shard_map/reduce_scatter | solution.py:122
  (20 shorter events, 0.2 us)
Async XLA Ops:
  6.5 1.1 copy-start
  6.5 64.7 %all-gather.2.cloned.1.call-start = ((), (), s32[]{:S(2)}) async-start(), calls=%async_computation.4 | async-start | bytes 2621440 | tf_op jit(solution)/shard_map/all_gather | solution.py:81
  8.4 8.9 %collective-permute-start = (bf16[256,1,128]{0,2,1:T(8,128)(2,1)S(1)}, bf16[256,1,128]{0,2,1:T(8,128)(2,1)S(1)}, u32[]{:S(2)}, u32[]{:S(2)}) collective-permute-start(bf16[256,1,128]{0,2,1:T(8,128)(2,1)S(1)} %get-tuple-element.13), channel_id=1, source_target_pairs={{0,4},{4,0},{8,12},{12,8},{16,20},{20,16},{24,28},{28,24},{1,5},{5... | collective-permute-start | bytes 196616 | tf_op jit(solution)/shard_map/ppermute | solution.py:26
  11.4 9.5 %collective-permute-start.1 = (bf16[256,1,128]{0,2,1:T(8,128)(2,1)S(1)}, bf16[256,1,128]{0,2,1:T(8,128)(2,1)S(1)}, u32[]{:S(2)}, u32[]{:S(2)}) collective-permute-start(bf16[256,1,128]{0,2,1:T(8,128)(2,1)S(1)} %get-tuple-element.12), channel_id=1, source_target_pairs={{0,8},{4,12},{8,0},{12,4},{16,24},{20,28},{24,16},{28,20},{1,9},{5... | collective-permute-start | bytes 196616 | tf_op jit(solution)/shard_map/ppermute | solution.py:26
  13.0 8.1 %collective-permute-start.2 = (bf16[256,1,128]{0,2,1:T(8,128)(2,1)S(1)}, bf16[256,1,128]{0,2,1:T(8,128)(2,1)S(1)}, u32[]{:S(2)}, u32[]{:S(2)}) collective-permute-start(bf16[256,1,128]{0,2,1:T(8,128)(2,1)S(1)} %get-tuple-element.11), channel_id=1, source_target_pairs={{0,12},{4,8},{8,4},{12,0},{16,28},{20,24},{24,20},{28,16},{1,13},{... | collective-permute-start | bytes 196616 | tf_op jit(solution)/shard_map/ppermute | solution.py:26
  13.0 8.1 %collective-permute-start.3 = (bf16[256,1,128]{0,2,1:T(8,128)(2,1)S(1)}, bf16[256,1,128]{0,2,1:T(8,128)(2,1)S(1)}, u32[]{:S(2)}, u32[]{:S(2)}) collective-permute-start(bf16[256,1,128]{0,2,1:T(8,128)(2,1)S(1)} %get-tuple-element.10), channel_id=1, source_target_pairs={{0,16},{4,20},{8,24},{12,28},{16,0},{20,4},{24,8},{28,12},{1,17},{... | collective-permute-start | bytes 196616 | tf_op jit(solution)/shard_map/ppermute | solution.py:26
  16.0 10.2 %collective-permute-start.4 = (bf16[256,1,128]{0,2,1:T(8,128)(2,1)S(1)}, bf16[256,1,128]{0,2,1:T(8,128)(2,1)S(1)}, u32[]{:S(2)}, u32[]{:S(2)}) collective-permute-start(bf16[256,1,128]{0,2,1:T(8,128)(2,1)S(1)} %get-tuple-element.9), channel_id=1, source_target_pairs={{0,20},{4,16},{8,28},{12,24},{16,4},{20,0},{24,12},{28,8},{1,21},{... | collective-permute-start | bytes 196616 | tf_op jit(solution)/shard_map/ppermute | solution.py:26
  17.3 8.9 %collective-permute-start.5 = (bf16[256,1,128]{0,2,1:T(8,128)(2,1)S(1)}, bf16[256,1,128]{0,2,1:T(8,128)(2,1)S(1)}, u32[]{:S(2)}, u32[]{:S(2)}) collective-permute-start(bf16[256,1,128]{0,2,1:T(8,128)(2,1)S(1)} %get-tuple-element.8), channel_id=1, source_target_pairs={{0,24},{4,28},{8,16},{12,20},{16,8},{20,12},{24,0},{28,4},{1,25},{... | collective-permute-start | bytes 196616 | tf_op jit(solution)/shard_map/ppermute | solution.py:26
  21.0 7.1 %collective-permute-start.6 = (bf16[256,1,128]{0,2,1:T(8,128)(2,1)S(1)}, bf16[256,1,128]{0,2,1:T(8,128)(2,1)S(1)}, u32[]{:S(2)}, u32[]{:S(2)}) collective-permute-start(bf16[256,1,128]{0,2,1:T(8,128)(2,1)S(1)} %get-tuple-element.7), channel_id=1, source_target_pairs={{0,28},{4,24},{8,20},{12,16},{16,12},{20,8},{24,4},{28,0},{1,29},{... | collective-permute-start | bytes 196616 | tf_op jit(solution)/shard_map/ppermute | solution.py:26
  29.3 10.3 %copy-start.2 = (bf16[128,23,64]{0,2,1:T(8,128)(2,1)S(1)}, bf16[128,23,64]{0,2,1:T(8,128)(2,1)}, u32[]{:S(2)}) copy-start(bf16[128,23,64]{0,2,1:T(8,128)(2,1)} %param.7) | copy-start | bytes 1130500
  39.6 5.2 %copy-start.5 = (s32[8]{0:T(128)S(1)}, s32[8]{0:T(128)}, u32[]{:S(2)}) copy-start(s32[8]{0:T(128)} %param.9) | copy-start | bytes 100
  39.6 5.3 %copy-start.1 = (bf16[128,8,256]{2,1,0:T(8,128)(2,1)S(1)}, bf16[128,8,256]{2,1,0:T(8,128)(2,1)}, u32[]{:S(2)}) copy-start(bf16[128,8,256]{2,1,0:T(8,128)(2,1)} %param.6) | copy-start | bytes 1572868
  40.9 12.6 %all-to-all-start.1 = ((bf16[128,8,128]{0,2,1:T(8,128)(2,1)}), bf16[128,8,128]{0,2,1:T(8,128)(2,1)S(1)}, u32[]{:S(2)}, u32[]{:S(2)}) async-start(bf16[128,8,128]{0,2,1:T(8,128)(2,1)} %bitcast.16), calls=%async_computation.1 | async-start | bytes 524288 | tf_op jit(solution)/shard_map/all_to_all | solution.py:69
  53.5 17.8 %all-to-all-start = ((bf16[128,8,256]{2,0,1:T(8,128)(2,1)}), bf16[128,8,256]{2,0,1:T(8,128)(2,1)S(1)}, u32[]{:S(2)}, u32[]{:S(2)}) async-start(bf16[128,8,256]{2,0,1:T(8,128)(2,1)} %copy.20), calls=%async_computation | async-start | bytes 1048576 | tf_op jit(solution)/shard_map/all_to_all | solution.py:70
  57.1 74.1 %reduce-scatter.3.cloned.1.call-start = ((), (), s32[]{:S(2)}) async-start(), calls=%async_computation.5 | async-start | bytes 327680 | tf_op jit(solution)/shard_map/reduce_scatter | solution.py:110
  71.2 0.8 copy-start.3
  110.6 1.3 copy-start.4
  111.9 86.5 %reduce-scatter.5.cloned.1.call-start = ((), (), s32[]{:S(2)}) async-start(), calls=%async_computation.6 | async-start | bytes 1695744 | tf_op jit(solution)/shard_map/reduce_scatter | solution.py:122
Sparse Core Ops, SparseCore 0:
  39.7 21.8 all-gather.1
  112.0 19.1 reduce-scatter.2
  134.6 63.6 reduce-scatter.4
